TPU v7x, 256 devices: a whole 4x4x8 slice. The times are simulated.
256 devices in a mesh: wide: 32 (over z, y), slab: 8 (over x, core).
Axes of the slice: x: 4, y: 4, z: 8, core: 2. Of those that a mesh axis runs over, the one named last changes fastest.
Arguments:
- thermal_state: float32 [32, 128, 32, 1024], P('wide', 'slab'), may hold values from -5 to 5
- thermal_spreading_rate: bfloat16 [32, 128, 32, 1024], P('wide', 'slab'), may hold values from 0.5 to 1.5
- flow_speed_vector: bfloat16 [3, 32, 128, 32, 1024], P(None, 'wide', 'slab'), may hold values from -0.796875 to 0.796875
- interface_guess: float32 [32, 2048], P('wide', 'slab'), may hold values from -4 to 4
- partner_facing_rows: int32 [32, 2048], P('wide', 'slab'), may hold values from 0 to 2047, each once within a row
- mismatch_change_matrix: float32 [32, 2048, 128], P('wide', 'slab'), may hold values from -5 to 5
- output_change_matrix: float32 [32, 2048, 128], P('wide', 'slab'), may hold values from -1.8 to 1.8
Outputs:
- temperature_out: float32 [32, 128, 32, 1024], P('wide', 'slab')
- updated_interface_guess: float32 [32, 2048], P('wide', 'slab')
- unitary_basis_factor: float32 [32, 2048, 128], P('wide', 'slab')
Inputs may be any that keep to these rules, and one draw needn't show every extreme that they name: `partner_facing_rows`: each partition's rows of matching are a permutation of its partner's interface rows.
All inputs are finite; a program needn't handle non-finite values.
Results may differ from a plain program's by a relative error of at most 0.0003.
Values may be sent and summed in bfloat16 or wider, within the bound.
No kernel may reach another device: no remote copies, remote signals or barrier semaphores. Data moves between devices by JAX's collectives and lax.ppermute only.
A program may use at most 64 MiB of HBM per device.

v0:
```python
import math
import jax
import jax.numpy as jnp
from jax import lax
from jax.sharding import PartitionSpec as P

INTERFACE_STRIP = 64
SWEEPS = 4
STEP_SIZE = 0.11


def padded(cells, sides, width):
    for axis, dim in sides:
        count = lax.axis_size(axis)
        ends = count - 1
        head = lax.slice_in_dim(cells, 0, width, axis=dim)
        tail = lax.slice_in_dim(cells, cells.shape[dim] - width, cells.shape[dim], axis=dim)
        cells = jnp.concatenate(
            [
                lax.ppermute(tail, axis, [(i, (i + 1) % count) for i in range(ends)]),
                cells,
                lax.ppermute(head, axis, [((i + 1) % count, i) for i in range(ends)]),
            ],
            axis=dim,
        )
    return cells


def partner(value, axis, stride):
    mask = 2**stride
    pairs = [(source, source ^ mask) for source in range(lax.axis_size(axis))]
    return lax.ppermute(value, axis, pairs)


def surround_wrapper(block_rows, mirror_layer):
    bottom = jnp.zeros((block_rows.shape[0], 1, block_rows.shape[2]), block_rows.dtype)
    stacked = jnp.concatenate([bottom, block_rows, mirror_layer[:, None, :]], axis=1)
    return jnp.pad(stacked, ((0, 0), (0, 0), (1, 1)))


def march_forward(bordered_array, diffuse_subdomain, subdomain_flow_speed):
    centre = bordered_array[1:-1, 1:-1, 1:-1]
    plus_first = bordered_array[2:, 1:-1, 1:-1]
    minus_first = bordered_array[:-2, 1:-1, 1:-1]
    plus_second = bordered_array[1:-1, 2:, 1:-1]
    minus_second = bordered_array[1:-1, :-2, 1:-1]
    plus_third = bordered_array[1:-1, 1:-1, 2:]
    minus_third = bordered_array[1:-1, 1:-1, :-2]
    spread = (
        plus_first
        + minus_first
        + plus_second
        + minus_second
        + plus_third
        + minus_third
        - 6.0 * centre
    )
    carried = 0.5 * (
        subdomain_flow_speed[0].astype(jnp.float32) * (plus_first - minus_first)
        + subdomain_flow_speed[1].astype(jnp.float32) * (plus_second - minus_second)
        + subdomain_flow_speed[2].astype(jnp.float32) * (plus_third - minus_third)
    )
    return centre + STEP_SIZE * (diffuse_subdomain.astype(jnp.float32) * spread - carried)


def shards(
    thermal_state,
    thermal_spreading_rate,
    flow_speed_vector,
    interface_guess,
    partner_facing_rows,
    mismatch_change_matrix,
    output_change_matrix,
):
    subdomain_thermal_state = thermal_state[0]
    diffuse_subdomain = thermal_spreading_rate[0]
    subdomain_flow_speed = flow_speed_vector[:, 0]
    layer_stack = subdomain_thermal_state.shape[0]
    vertical_extent = subdomain_thermal_state.shape[1]
    rows_dev = interface_guess.shape[1]
    mirror_layer = jnp.repeat(interface_guess[0].reshape(layer_stack, -1), INTERFACE_STRIP, axis=1)
    panel = mismatch_change_matrix[0]
    gram_local = lax.dot_general(
        panel,
        panel,
        (((0,), (0,)), ((), ())),
        precision=lax.Precision.HIGHEST,
        preferred_element_type=jnp.float32,
    )
    ghost_padded = jnp.pad(mirror_layer, ((1, 1), (0, 0)))
    for sweep in range(SWEEPS):
        widened_array = padded(subdomain_thermal_state, (("slab", 0),), 1)
        subdomain_thermal_state = march_forward(
            surround_wrapper(widened_array, ghost_padded), diffuse_subdomain, subdomain_flow_speed
        )
    face_means = jnp.mean(
        subdomain_thermal_state[:, vertical_extent - 1, :].reshape(
            layer_stack, -1, INTERFACE_STRIP
        ),
        axis=2,
    )
    face_means = face_means.reshape(1, rows_dev)
    top_bit = lax.axis_size("wide").bit_length() - 2
    partner_own = partner(face_means, "wide", top_bit)
    partner_all = lax.all_gather(partner_own, "slab", axis=1, tiled=True)
    tilde = jnp.take(partner_all[0], partner_facing_rows[0], axis=0)
    resid = tilde - interface_guess[0]
    proj_local = jnp.dot(
        resid, panel, precision=lax.Precision.HIGHEST, preferred_element_type=jnp.float32
    )
    gram_matrix, projection = lax.psum((gram_local, proj_local), ("wide", "slab"))
    lower_factor = jnp.linalg.cholesky(gram_matrix)
    half_solve = lax.linalg.triangular_solve(
        lower_factor, projection[:, None], left_side=True, lower=True
    )
    coefficients = -lax.linalg.triangular_solve(
        lower_factor, half_solve, left_side=True, lower=True, transpose_a=True
    )[:, 0]
    update = jnp.dot(
        output_change_matrix[0],
        coefficients,
        precision=lax.Precision.HIGHEST,
        preferred_element_type=jnp.float32,
    )
    updated_interface_guess = tilde + update
    total_rows = rows_dev * lax.axis_size("slab") * lax.axis_size("wide")
    scaled = lax.linalg.triangular_solve(
        lower_factor, panel, left_side=False, lower=True, transpose_a=True
    )
    unitary_basis_factor = math.sqrt(total_rows) * scaled
    return (
        subdomain_thermal_state[None],
        updated_interface_guess[None],
        unitary_basis_factor[None],
    )


def solution(mesh):
    return jax.shard_map(
        shards,
        mesh=mesh,
        in_specs=(
            P("wide", "slab", None, None),
            P("wide", "slab", None, None),
            P(None, "wide", "slab", None, None),
            P("wide", "slab"),
            P("wide", "slab"),
            P("wide", "slab", None),
            P("wide", "slab", None),
        ),
        out_specs=(P("wide", "slab", None, None), P("wide", "slab"), P("wide", "slab", None)),
        check_vma=False,
    )
```

profile of v0, /device:TPU:1, one launch (start us, length us, event | category | flops | bytes accessed | tf_op | source)
XLA Modules:
  0.0 438.8 jit_solution(339822084845978649)
XLA Ops:
  7.2 1.0 slice_bitcast_fusion
  8.2 5.1 %collective-permute-start = (f32[1,32,1024]{2,1,0:T(8,128)S(1)}, f32[1,32,1024]{2,1,0:T(8,128)S(1)}, u32[]{:S(2)}, u32[]{:S(2)}) collective-permute-start(f32[1,32,1024]{2,1,0:T(8,128)S(1)} %get-tuple-element.16), channel_id=1, source_target_pairs={{1,0},{2,1},{3,2},{4,3},{5,4},{6,5},{7,6},{9,8},{10,9},{11,10},{12... | collective-permute-start | bytes 393224 | tf_op jit(solution)/shard_map/ppermute | solution.py:22
  13.4 1.9 collective-permute-start.1
  15.3 1.0 fusion.39
  17.6 1.3 reduce.11
  19.3 237.0 %all-reduce.11.cloned.1.call-done = f32[128,128]{0,1:T(8,128)} async-done(((f32[128,128]{0,1:T(8,128)}), f32[128,128]{0,1:T(8,128)}) %all-reduce.11.cloned.1.call-update) | async-done | bytes 65552 | tf_op jit(solution)/shard_map/psum | solution.py:111
  256.3 0.9 copy.14
  257.9 2.3 pad_maximum_fusion.3
  260.7 7.0 %fusion.2 = f32[16,32,1024]{2,1,0:T(8,128)S(1)} fusion(f32[16,32,1024]{2,1,0:T(8,128)} %bitcast.90, f32[18,34,1024]{2,1,0:T(8,128)S(1)} %pad_maximum_fusion.3, f32[1,32,1024]{2,1,0:T(8,128)S(1)} %collective-permute-done, f32[1,32,1024]{2,1,0:T(8,128)S(1)} %copy-done.11, f32[18,1,1024]{2,1,0:T(1,128)S(1)} %broadcast_in_dim.30, ...), kind=kLoop, calls=%fused_computation.35 | loop fusion | flops 18874368 | bytes 11231232 | tf_op jit(solution)/shard_map/add | solution.py:63
  267.8 1.3 copy-done.4
  269.8 1.9 collective-permute-start.2
  271.7 3.6 collective-permute-start.3
  276.0 12.5 %cholesky.16 = f32[128,128]{1,0:T(8,128)S(1)} custom-call(f32[128,128]{1,0:T(8,128)} %fusion.45), custom_call_target="Cholesky" | custom-call | tf_op jit(solution)/shard_map/jit(cholesky)/cholesky | solution.py:112
  288.6 2.3 pad_maximum_fusion.2
  291.1 4.6 %fusion.5 = f32[16,32,1024]{2,1,0:T(8,128)S(1)} fusion(f32[16,32,1024]{2,1,0:T(8,128)S(1)} %copy-done.5, f32[18,34,1024]{2,1,0:T(8,128)S(1)} %pad_maximum_fusion.2, f32[1,32,1024]{2,1,0:T(8,128)S(1)} %collective-permute-done.2, f32[1,32,1024]{2,1,0:T(8,128)} %collective-permute-done.3, f32[18,1,1024]{2,1,0:T(1,128)S(1)} %broadcast_in_dim.30, ...), kind=kLoop, calls=%fused_computation.38 | loop fusion | flops 18874368 | bytes 11231232 | tf_op jit(solution)/shard_map/add | solution.py:63
  295.8 1.9 collective-permute-start.4
  297.7 3.8 collective-permute-start.5
  302.2 1.1 collective-permute-done.5
  304.0 5.4 %fusion.8 = f32[16,32,1024]{2,1,0:T(8,128)S(1)} fusion(f32[16,32,1024]{2,1,0:T(8,128)S(1)} %fusion.5, f32[18,34,1024]{2,1,0:T(8,128)S(1)} %pad_maximum_fusion.1, f32[1,32,1024]{2,1,0:T(8,128)S(1)} %collective-permute-done.4, f32[1,32,1024]{2,1,0:T(8,128)S(1)} %collective-permute-done.5, f32[18,1,1024]{2,1,0:T(1,128)S(1)} %broadcast_in_dim.30, ...), kind=kLoop, calls=%fused_computation.41 | loop fusion | flops 18874368 | bytes 11231232 | tf_op jit(solution)/shard_map/add | solution.py:63
  309.4 1.3 copy-done.2
  311.4 1.9 collective-permute-start.6
  313.3 4.4 collective-permute-start.7
  317.7 1.3 fusion.41
  319.0 10.6 %custom-call.10 = f32[1,128,128]{1,2,0:T(8,128)S(1)} custom-call(f32[1,128,128]{2,1,0:T(8,128)} %fusion.41), custom_call_target="InvertDiagBlocksLowerTriangular" | custom-call | tf_op jit(solution)/shard_map/triangular_solve | solution.py:116
  329.7 2.3 pad_maximum_fusion
  332.2 4.6 %fusion.11 = f32[16,32,1024]{2,1,0:T(8,128)S(1)} fusion(f32[16,32,1024]{2,1,0:T(8,128)S(1)} %copy-done.3, f32[18,34,1024]{2,1,0:T(8,128)S(1)} %pad_maximum_fusion, f32[1,32,1024]{2,1,0:T(8,128)S(1)} %collective-permute-done.6, f32[1,32,1024]{2,1,0:T(8,128)} %collective-permute-done.7, f32[18,1,1024]{2,1,0:T(1,128)S(1)} %broadcast_in_dim.30, ...), kind=kLoop, calls=%fused_computation.44 | loop fusion | flops 18874368 | bytes 11231232 | tf_op jit(solution)/shard_map/add | solution.py:63
  336.8 1.3 copy-done.9
  338.6 0.9 collective-permute-start.8
  340.6 4.4 %collective-permute-done.8 = f32[1,256]{1,0:T(1,128)S(1)} collective-permute-done((f32[1,256]{1,0:T(1,128)S(1)}, f32[1,256]{1,0:T(1,128)S(1)}, u32[]{:S(2)}, u32[]{:S(2)}) %collective-permute-start.8) | collective-permute-done | bytes 1056 | tf_op jit(solution)/shard_map/ppermute | solution.py:32
  345.0 10.1 %all_gather.3 = f32[1,2048]{1,0:T(1,128)S(1)} all-gather(f32[1,256]{1,0:T(1,128)S(1)} %collective-permute-done.8), channel_id=1, replica_groups=mesh['wide'=32,'slab'=8] {'slab'}, dimensions={1}, use_global_device_ids=true | all-gather | bytes 9216 | tf_op jit(solution)/shard_map/all_gather | solution.py:105
  355.1 1.7 gather_fusion
  357.0 73.7 %psum.15 = f32[128]{0:T(128)S(1)} all-reduce(f32[128]{0:T(128)S(1)} %convolution_bitcast_fusion.2), channel_id=1, replica_groups=mesh['wide'=32,'slab'=8] {'wide','slab'}, use_global_device_ids=true, to_apply=%region_4.5 | all-reduce | flops 128 | bytes 1024 | tf_op jit(solution)/shard_map/psum | solution.py:111
  (70 shorter events, 9.6 us)
Async XLA Ops:
  7.2 8.2 %copy-start = (f32[1,256,128]{2,1,0:T(8,128)S(1)}, f32[1,256,128]{2,1,0:T(8,128)}, u32[]{:S(2)}) copy-start(f32[1,256,128]{2,1,0:T(8,128)} %param.12) | copy-start | bytes 393220
  7.2 249.1 %all-reduce.11.cloned.1.call-start = ((), (), s32[]{:S(2)}) async-start(), calls=%async_computation | async-start | bytes 131072 | tf_op jit(solution)/shard_map/psum | solution.py:111
  8.2 249.0 %collective-permute-start = (f32[1,32,1024]{2,1,0:T(8,128)S(1)}, f32[1,32,1024]{2,1,0:T(8,128)S(1)}, u32[]{:S(2)}, u32[]{:S(2)}) collective-permute-start(f32[1,32,1024]{2,1,0:T(8,128)S(1)} %get-tuple-element.16), channel_id=1, source_target_pairs={{1,0},{2,1},{3,2},{4,3},{5,4},{6,5},{7,6},{9,8},{10,9},{11,10},{12... | collective-permute-start | bytes 393224 | tf_op jit(solution)/shard_map/ppermute | solution.py:22
  13.4 243.8 %collective-permute-start.1 = (f32[1,32,1024]{2,1,0:T(8,128)S(1)}, f32[1,32,1024]{2,1,0:T(8,128)S(1)}, u32[]{:S(2)}, u32[]{:S(2)}) collective-permute-start(f32[1,32,1024]{2,1,0:T(8,128)S(1)} %get-tuple-element.15), channel_id=1, source_target_pairs={{0,1},{1,2},{2,3},{3,4},{4,5},{5,6},{6,7},{8,9},{9,10},{10,11},{11... | collective-permute-start | bytes 393224 | tf_op jit(solution)/shard_map/ppermute | solution.py:20
  257.2 0.7 copy-start.10
  257.9 2.6 copy-start.1
  257.9 2.8 copy-start.6
  257.9 2.8 copy-start.11
  260.7 14.6 %copy-start.12 = (f32[128,128]{0,1:T(8,128)S(1)}, f32[128,128]{0,1:T(8,128)}, u32[]{:S(2)}) copy-start(f32[128,128]{0,1:T(8,128)} %all-reduce.11.cloned.1.call-done) | copy-start | bytes 196612
  267.8 1.3 copy-start.4
  269.8 18.8 %collective-permute-start.2 = (f32[1,32,1024]{2,1,0:T(8,128)}, f32[1,32,1024]{2,1,0:T(8,128)S(1)}, u32[]{:S(2)}, u32[]{:S(2)}) collective-permute-start(f32[1,32,1024]{2,1,0:T(8,128)} %get-tuple-element.14), channel_id=1, source_target_pairs={{1,0},{2,1},{3,2},{4,3},{5,4},{6,5},{7,6},{9,8},{10,9},{11,10},{12... | collective-permute-start | bytes 393224 | tf_op jit(solution)/shard_map/ppermute | solution.py:22
  271.7 16.9 %collective-permute-start.3 = (f32[1,32,1024]{2,1,0:T(8,128)}, f32[1,32,1024]{2,1,0:T(8,128)}, u32[]{:S(2)}, u32[]{:S(2)}) collective-permute-start(f32[1,32,1024]{2,1,0:T(8,128)} %get-tuple-element.13), channel_id=1, source_target_pairs={{0,1},{1,2},{2,3},{3,4},{4,5},{5,6},{6,7},{8,9},{9,10},{10,11},{11... | collective-permute-start | bytes 393224 | tf_op jit(solution)/shard_map/ppermute | solution.py:20
  288.6 13.0 %copy-start.13 = (f32[128,128]{1,0:T(8,128)}, f32[128,128]{1,0:T(8,128)S(1)}, u32[]{:S(2)}) copy-start(f32[128,128]{1,0:T(8,128)S(1)} %cholesky.16) | copy-start | bytes 196612
  288.6 2.3 copy-start.5
  288.6 2.5 copy-start.7
  295.8 6.4 %collective-permute-start.4 = (f32[1,32,1024]{2,1,0:T(8,128)S(1)}, f32[1,32,1024]{2,1,0:T(8,128)S(1)}, u32[]{:S(2)}, u32[]{:S(2)}) collective-permute-start(f32[1,32,1024]{2,1,0:T(8,128)S(1)} %get-tuple-element.12), channel_id=1, source_target_pairs={{1,0},{2,1},{3,2},{4,3},{5,4},{6,5},{7,6},{9,8},{10,9},{11,10},{12... | collective-permute-start | bytes 393224 | tf_op jit(solution)/shard_map/ppermute | solution.py:22
  297.7 5.6 %collective-permute-start.5 = (f32[1,32,1024]{2,1,0:T(8,128)S(1)}, f32[1,32,1024]{2,1,0:T(8,128)S(1)}, u32[]{:S(2)}, u32[]{:S(2)}) collective-permute-start(f32[1,32,1024]{2,1,0:T(8,128)S(1)} %get-tuple-element.11), channel_id=1, source_target_pairs={{0,1},{1,2},{2,3},{3,4},{4,5},{5,6},{6,7},{8,9},{9,10},{10,11},{11... | collective-permute-start | bytes 393224 | tf_op jit(solution)/shard_map/ppermute | solution.py:20
  304.0 13.7 %copy-start.14 = (f32[128,128]{1,0:T(8,128)S(1)}, f32[128,128]{1,0:T(8,128)}, u32[]{:S(2)}) copy-start(f32[128,128]{1,0:T(8,128)} %copy-done.13) | copy-start | bytes 196612
  309.4 1.3 copy-start.2
  311.4 18.2 %collective-permute-start.6 = (f32[1,32,1024]{2,1,0:T(8,128)}, f32[1,32,1024]{2,1,0:T(8,128)S(1)}, u32[]{:S(2)}, u32[]{:S(2)}) collective-permute-start(f32[1,32,1024]{2,1,0:T(8,128)} %get-tuple-element.10), channel_id=1, source_target_pairs={{1,0},{2,1},{3,2},{4,3},{5,4},{6,5},{7,6},{9,8},{10,9},{11,10},{12... | collective-permute-start | bytes 393224 | tf_op jit(solution)/shard_map/ppermute | solution.py:22
  313.3 16.3 %collective-permute-start.7 = (f32[1,32,1024]{2,1,0:T(8,128)}, f32[1,32,1024]{2,1,0:T(8,128)}, u32[]{:S(2)}, u32[]{:S(2)}) collective-permute-start(f32[1,32,1024]{2,1,0:T(8,128)} %get-tuple-element.9), channel_id=1, source_target_pairs={{0,1},{1,2},{2,3},{3,4},{4,5},{5,6},{6,7},{8,9},{9,10},{10,11},{11... | collective-permute-start | bytes 393224 | tf_op jit(solution)/shard_map/ppermute | solution.py:20
  329.6 2.3 copy-start.3
  329.7 2.5 copy-start.8
  336.8 1.3 copy-start.9
  338.2 18.6 %copy-start.16 = (s32[1,256]{1,0:T(1,128)S(1)}, s32[1,256]{1,0:T(1,128)}, u32[]{:S(2)}) copy-start(s32[1,256]{1,0:T(1,128)} %param.11) | copy-start | bytes 3076
  338.2 18.6 %copy-start.17 = (f32[1,256]{1,0:T(1,128)S(1)}, f32[1,256]{1,0:T(1,128)}, u32[]{:S(2)}) copy-start(f32[1,256]{1,0:T(1,128)} %param.10) | copy-start | bytes 3076
  338.2 92.9 %copy-start.15 = (f32[1,256,128]{2,1,0:T(8,128)S(1)}, f32[1,256,128]{2,1,0:T(8,128)}, u32[]{:S(2)}) copy-start(f32[1,256,128]{2,1,0:T(8,128)} %param.13) | copy-start | bytes 393220
  338.6 6.4 %collective-permute-start.8 = (f32[1,256]{1,0:T(1,128)S(1)}, f32[1,256]{1,0:T(1,128)S(1)}, u32[]{:S(2)}, u32[]{:S(2)}) collective-permute-start(f32[1,256]{1,0:T(1,128)S(1)} %div.18), channel_id=1, source_target_pairs={{0,128},{8,136},{16,144},{24,152},{32,160},{40,168},{48,176},{56,1... | collective-permute-start | bytes 3080 | tf_op jit(solution)/shard_map/ppermute | solution.py:32
Sparse Core Ops, SparseCore 0:
  16.5 239.7 all-reduce.10
where the time goes:
time: 439 us
  waiting for transfers between devices  242 us (55%)
  blocking collectives  83.8 us (19%)
  other arithmetic  57.7 us (13%)
  starting transfers between devices  25.5 us (6%)
  between operations  14.5 us (3%)
  local copies, waits for them, and re-layouts  12.7 us (3%)
    psum x1, waiting for transfers between devices, shards(): lax.psum((gram_local, proj_local), ('wide', 'slab'))  237 us
    psum x1, blocking collectives, shards(): lax.psum((gram_local, proj_local), ('wide', 'slab'))  73.7 us
    add x4, other arithmetic, march_forward(): centre + STEP_SIZE * (diffuse_subdomain.astype(jnp.float32) * spread - ca...  21.7 us
    ppermute x4, starting transfers between devices, padded(): lax.ppermute(tail, axis, [(i, (i + 1) % count) for i in range(ends)])  13.7 us
    another operation x3, other arithmetic, shards(): lower_factor = jnp.linalg.cholesky(gram_matrix)  13.2 us
    another operation x2, other arithmetic, shards(): lax.linalg.triangular_solve(lower_factor, half_solve, left_side=True, low...  11.9 us
    ppermute x4, starting transfers between devices, padded(): lax.ppermute(head, axis, [((i + 1) % count, i) for i in range(ends)])  10.9 us
    all_gather x1, blocking collectives, shards(): partner_all = lax.all_gather(partner_own, 'slab', axis=1, tiled=True)  10.1 us
  transfers between devices with their start and end apart: 10, of which 3 were waited for; matrix products, arithmetic and copies ran while one was open for 7% of the time, Pallas kernels for 0%

commit v1 on v0

--- a/solution.py
+++ b/solution.py
@@ -102,7 +102,15 @@
     face_means = face_means.reshape(1, rows_dev)
     top_bit = lax.axis_size("wide").bit_length() - 2
     partner_own = partner(face_means, "wide", top_bit)
-    partner_all = lax.all_gather(partner_own, "slab", axis=1, tiled=True)
+    partner_all = jnp.concatenate(
+        lax.all_to_all(
+            jnp.stack([partner_own for _ in range(lax.axis_size("slab"))]),
+            axis_name="slab",
+            split_axis=0,
+            concat_axis=0,
+        ),
+        axis=1,
+    )
     tilde = jnp.take(partner_all[0], partner_facing_rows[0], axis=0)
     resid = tilde - interface_guess[0]
     proj_local = jnp.dot(

time: 439 us -> 417 us (0.950)
  waiting for transfers between devices: 242 us -> 224 us
  blocking collectives: 83.8 us -> 75.5 us
  starting transfers between devices: 25.5 us -> 30.7 us
    psum x1, waiting for transfers between devices: 237 us -> 219 us  [shards(): lax.psum((gram_local, proj_local), ('wide', 'slab'))]
    all_gather x1 -> x0, blocking collectives: 10.1 us -> none  [shards(): partner_all = lax.all_gather(partner_own, 'slab', axis=1, tiled=True)]
    all_to_all x0 -> x1, starting transfers between devices: none -> 5.69 us  [shards(): lax.all_to_all(jnp.stack([partner_own for _ in range(lax.axis_size('slab'...]
    ppermute x1, waiting for transfers between devices: 4.4 us -> 0.01 us  [partner(): return lax.ppermute(value, axis, pairs)]
  transfers between devices with their start and end apart: 10 -> 11, of which waited for: 3 -> 3; matrix products, arithmetic and copies ran while one was open for 7% -> 10% of each run, Pallas kernels for 0% -> 0%
where the time goes in v1:
time: 417 us; the launch traced here: 416 us
  waiting for transfers between devices  224 us (54%)
  blocking collectives  75.5 us (18%)
  other arithmetic  56.2 us (13%)
  starting transfers between devices  30.7 us (7%)
  between operations  14.5 us (3%)
  local copies, waits for them, and re-layouts  13.4 us (3%)
    psum x1, waiting for transfers between devices, shards(): lax.psum((gram_local, proj_local), ('wide', 'slab'))  219 us
    psum x1, blocking collectives, shards(): lax.psum((gram_local, proj_local), ('wide', 'slab'))  75.5 us
    add x4, other arithmetic, march_forward(): centre + STEP_SIZE * (diffuse_subdomain.astype(jnp.float32) * spread - ca...  21.7 us
    another operation x3, other arithmetic, shards(): lower_factor = jnp.linalg.cholesky(gram_matrix)  13.2 us
    ppermute x4, starting transfers between devices, padded(): lax.ppermute(tail, axis, [(i, (i + 1) % count) for i in range(ends)])  12.5 us
    ppermute x4, starting transfers between devices, padded(): lax.ppermute(head, axis, [((i + 1) % count, i) for i in range(ends)])  11.4 us
    another operation x2, other arithmetic, shards(): lax.linalg.triangular_solve(lower_factor, half_solve, left_side=True, low...  10.5 us
  transfers between devices with their start and end apart: 11, of which 3 were waited for; matrix products, arithmetic and copies ran while one was open for 10% of the time, Pallas kernels for 0%

profile of v1, /device:TPU:1, one launch (start us, length us, event | category | flops | bytes accessed | tf_op | source)
XLA Modules:
  0.0 416.2 jit_solution(12706895130356017373)
XLA Ops:
  7.2 1.0 slice_bitcast_fusion
  8.2 5.1 %collective-permute-start = (f32[1,32,1024]{2,1,0:T(8,128)S(1)}, f32[1,32,1024]{2,1,0:T(8,128)S(1)}, u32[]{:S(2)}, u32[]{:S(2)}) collective-permute-start(f32[1,32,1024]{2,1,0:T(8,128)S(1)} %get-tuple-element.16), channel_id=1, source_target_pairs={{1,0},{2,1},{3,2},{4,3},{5,4},{6,5},{7,6},{9,8},{10,9},{11,10},{12... | collective-permute-start | bytes 393224 | tf_op jit(solution)/shard_map/ppermute | solution.py:22
  13.4 1.9 collective-permute-start.1
  15.3 1.0 fusion.39
  16.9 1.3 reduce.11
  19.3 2.3 pad_maximum_fusion.3
  22.1 7.0 %fusion.2 = f32[16,32,1024]{2,1,0:T(8,128)S(1)} fusion(f32[16,32,1024]{2,1,0:T(8,128)} %bitcast.91, f32[18,34,1024]{2,1,0:T(8,128)S(1)} %pad_maximum_fusion.3, f32[1,32,1024]{2,1,0:T(8,128)S(1)} %collective-permute-done, f32[1,32,1024]{2,1,0:T(8,128)S(1)} %copy-done.11, f32[18,1,1024]{2,1,0:T(1,128)S(1)} %broadcast_in_dim.30, ...), kind=kLoop, calls=%fused_computation.35 | loop fusion | flops 18874368 | bytes 11231232 | tf_op jit(solution)/shard_map/add | solution.py:63
  29.1 1.3 copy-done.2
  31.2 2.4 collective-permute-start.2
  33.6 3.2 collective-permute-start.3
  37.3 219.0 %all-reduce.11.cloned.1.call-done = f32[128,128]{0,1:T(8,128)} async-done(((f32[128,128]{0,1:T(8,128)}), f32[128,128]{0,1:T(8,128)}) %all-reduce.11.cloned.1.call-update) | async-done | bytes 65552 | tf_op jit(solution)/shard_map/psum | solution.py:119
  256.3 0.9 copy.14
  257.3 2.3 pad_maximum_fusion.2
  259.8 4.7 %fusion.5 = f32[16,32,1024]{2,1,0:T(8,128)S(1)} fusion(f32[16,32,1024]{2,1,0:T(8,128)S(1)} %copy-done.3, f32[18,34,1024]{2,1,0:T(8,128)S(1)} %pad_maximum_fusion.2, f32[1,32,1024]{2,1,0:T(8,128)S(1)} %collective-permute-done.2, f32[1,32,1024]{2,1,0:T(8,128)} %collective-permute-done.3, f32[18,1,1024]{2,1,0:T(1,128)S(1)} %broadcast_in_dim.30, ...), kind=kLoop, calls=%fused_computation.38 | loop fusion | flops 18874368 | bytes 11231232 | tf_op jit(solution)/shard_map/add | solution.py:63
  264.5 1.3 copy-done.4
  266.5 1.9 collective-permute-start.4
  268.4 3.8 collective-permute-start.5
  272.9 12.5 %cholesky.16 = f32[128,128]{1,0:T(8,128)S(1)} custom-call(f32[128,128]{1,0:T(8,128)} %fusion.45), custom_call_target="Cholesky" | custom-call | tf_op jit(solution)/shard_map/jit(cholesky)/cholesky | solution.py:120
  285.5 2.3 pad_maximum_fusion.1
  288.0 4.6 %fusion.8 = f32[16,32,1024]{2,1,0:T(8,128)S(1)} fusion(f32[16,32,1024]{2,1,0:T(8,128)S(1)} %copy-done.5, f32[18,34,1024]{2,1,0:T(8,128)S(1)} %pad_maximum_fusion.1, f32[1,32,1024]{2,1,0:T(8,128)S(1)} %collective-permute-done.4, f32[1,32,1024]{2,1,0:T(8,128)} %collective-permute-done.5, f32[18,1,1024]{2,1,0:T(1,128)S(1)} %broadcast_in_dim.30, ...), kind=kLoop, calls=%fused_computation.41 | loop fusion | flops 18874368 | bytes 11231232 | tf_op jit(solution)/shard_map/add | solution.py:63
  292.7 1.9 collective-permute-start.6
  294.6 3.6 collective-permute-start.7
  298.9 1.2 collective-permute-done.7
  300.8 5.4 %fusion.11 = f32[16,32,1024]{2,1,0:T(8,128)S(1)} fusion(f32[16,32,1024]{2,1,0:T(8,128)S(1)} %fusion.8, f32[18,34,1024]{2,1,0:T(8,128)S(1)} %pad_maximum_fusion, f32[1,32,1024]{2,1,0:T(8,128)S(1)} %collective-permute-done.6, f32[1,32,1024]{2,1,0:T(8,128)S(1)} %collective-permute-done.7, f32[18,1,1024]{2,1,0:T(1,128)S(1)} %broadcast_in_dim.30, ...), kind=kLoop, calls=%fused_computation.44 | loop fusion | flops 18874368 | bytes 11231232 | tf_op jit(solution)/shard_map/add | solution.py:63
  306.3 1.3 copy-done.9
  308.0 1.1 collective-permute-start.8
  309.8 9.8 %custom-call.10 = f32[1,128,128]{1,2,0:T(8,128)S(1)} custom-call(f32[1,128,128]{2,1,0:T(8,128)S(1)} %fusion.41), custom_call_target="InvertDiagBlocksLowerTriangular" | custom-call | tf_op jit(solution)/shard_map/triangular_solve | solution.py:124
  320.2 5.7 %all-to-all-start = ((f32[8,1,256]{2,1,0:T(1,128)}), f32[8,1,256]{2,1,0:T(1,128)S(1)}, u32[]{:S(2)}, u32[]{:S(2)}) async-start(f32[8,1,256]{2,1,0:T(1,128)} %stack.2), calls=%async_computation | async-start | bytes 16384 | tf_op jit(solution)/shard_map/all_to_all | solution.py:106
  326.2 0.8 copy.15
  327.0 3.5 all-to-all-done
  330.5 1.9 gather_fusion
  332.6 75.5 %psum.15 = f32[128]{0:T(128)S(1)} all-reduce(f32[128]{0:T(128)S(1)} %convolution_bitcast_fusion.2), channel_id=1, replica_groups=mesh['wide'=32,'slab'=8] {'wide','slab'}, use_global_device_ids=true, to_apply=%region_4.5 | all-reduce | flops 128 | bytes 1024 | tf_op jit(solution)/shard_map/psum | solution.py:119
  (68 shorter events, 10.0 us)
Async XLA Ops:
  7.2 8.2 %copy-start = (f32[1,256,128]{2,1,0:T(8,128)S(1)}, f32[1,256,128]{2,1,0:T(8,128)}, u32[]{:S(2)}) copy-start(f32[1,256,128]{2,1,0:T(8,128)} %param.12) | copy-start | bytes 393220
  7.2 249.1 %all-reduce.11.cloned.1.call-start = ((), (), s32[]{:S(2)}) async-start(), calls=%async_computation.1 | async-start | bytes 131072 | tf_op jit(solution)/shard_map/psum | solution.py:119
  8.2 10.4 %collective-permute-start = (f32[1,32,1024]{2,1,0:T(8,128)S(1)}, f32[1,32,1024]{2,1,0:T(8,128)S(1)}, u32[]{:S(2)}, u32[]{:S(2)}) collective-permute-start(f32[1,32,1024]{2,1,0:T(8,128)S(1)} %get-tuple-element.16), channel_id=1, source_target_pairs={{1,0},{2,1},{3,2},{4,3},{5,4},{6,5},{7,6},{9,8},{10,9},{11,10},{12... | collective-permute-start | bytes 393224 | tf_op jit(solution)/shard_map/ppermute | solution.py:22
  13.4 5.2 %collective-permute-start.1 = (f32[1,32,1024]{2,1,0:T(8,128)S(1)}, f32[1,32,1024]{2,1,0:T(8,128)S(1)}, u32[]{:S(2)}, u32[]{:S(2)}) collective-permute-start(f32[1,32,1024]{2,1,0:T(8,128)S(1)} %get-tuple-element.15), channel_id=1, source_target_pairs={{0,1},{1,2},{2,3},{3,4},{4,5},{5,6},{6,7},{8,9},{9,10},{10,11},{11... | collective-permute-start | bytes 393224 | tf_op jit(solution)/shard_map/ppermute | solution.py:20
  18.6 0.7 copy-start.10
  19.3 2.6 copy-start.1
  19.3 2.8 copy-start.6
  19.3 2.8 copy-start.11
  22.1 14.6 %copy-start.14 = (s32[1,256]{1,0:T(1,128)S(1)}, s32[1,256]{1,0:T(1,128)}, u32[]{:S(2)}) copy-start(s32[1,256]{1,0:T(1,128)} %param.11) | copy-start | bytes 3076
  29.1 1.3 copy-start.2
  31.2 226.1 %collective-permute-start.2 = (f32[1,32,1024]{2,1,0:T(8,128)}, f32[1,32,1024]{2,1,0:T(8,128)S(1)}, u32[]{:S(2)}, u32[]{:S(2)}) collective-permute-start(f32[1,32,1024]{2,1,0:T(8,128)} %get-tuple-element.14), channel_id=1, source_target_pairs={{1,0},{2,1},{3,2},{4,3},{5,4},{6,5},{7,6},{9,8},{10,9},{11,10},{12... | collective-permute-start | bytes 393224 | tf_op jit(solution)/shard_map/ppermute | solution.py:22
  33.6 223.7 %collective-permute-start.3 = (f32[1,32,1024]{2,1,0:T(8,128)}, f32[1,32,1024]{2,1,0:T(8,128)}, u32[]{:S(2)}, u32[]{:S(2)}) collective-permute-start(f32[1,32,1024]{2,1,0:T(8,128)} %get-tuple-element.13), channel_id=1, source_target_pairs={{0,1},{1,2},{2,3},{3,4},{4,5},{5,6},{6,7},{8,9},{9,10},{10,11},{11... | collective-permute-start | bytes 393224 | tf_op jit(solution)/shard_map/ppermute | solution.py:20
  257.2 2.3 copy-start.3
  257.3 2.5 copy-start.7
  259.8 12.5 %copy-start.12 = (f32[128,128]{0,1:T(8,128)S(1)}, f32[128,128]{0,1:T(8,128)}, u32[]{:S(2)}) copy-start(f32[128,128]{0,1:T(8,128)} %all-reduce.11.cloned.1.call-done) | copy-start | bytes 196612
  264.5 1.3 copy-start.4
  266.5 19.0 %collective-permute-start.4 = (f32[1,32,1024]{2,1,0:T(8,128)}, f32[1,32,1024]{2,1,0:T(8,128)S(1)}, u32[]{:S(2)}, u32[]{:S(2)}) collective-permute-start(f32[1,32,1024]{2,1,0:T(8,128)} %get-tuple-element.12), channel_id=1, source_target_pairs={{1,0},{2,1},{3,2},{4,3},{5,4},{6,5},{7,6},{9,8},{10,9},{11,10},{12... | collective-permute-start | bytes 393224 | tf_op jit(solution)/shard_map/ppermute | solution.py:22
  268.4 17.1 %collective-permute-start.5 = (f32[1,32,1024]{2,1,0:T(8,128)}, f32[1,32,1024]{2,1,0:T(8,128)}, u32[]{:S(2)}, u32[]{:S(2)}) collective-permute-start(f32[1,32,1024]{2,1,0:T(8,128)} %get-tuple-element.11), channel_id=1, source_target_pairs={{0,1},{1,2},{2,3},{3,4},{4,5},{5,6},{6,7},{8,9},{9,10},{10,11},{11... | collective-permute-start | bytes 393224 | tf_op jit(solution)/shard_map/ppermute | solution.py:20
  285.4 2.3 copy-start.5
  285.5 2.5 copy-start.8
  292.7 6.3 %collective-permute-start.6 = (f32[1,32,1024]{2,1,0:T(8,128)S(1)}, f32[1,32,1024]{2,1,0:T(8,128)S(1)}, u32[]{:S(2)}, u32[]{:S(2)}) collective-permute-start(f32[1,32,1024]{2,1,0:T(8,128)S(1)} %get-tuple-element.10), channel_id=1, source_target_pairs={{1,0},{2,1},{3,2},{4,3},{5,4},{6,5},{7,6},{9,8},{10,9},{11,10},{12... | collective-permute-start | bytes 393224 | tf_op jit(solution)/shard_map/ppermute | solution.py:22
  294.6 5.6 %collective-permute-start.7 = (f32[1,32,1024]{2,1,0:T(8,128)S(1)}, f32[1,32,1024]{2,1,0:T(8,128)S(1)}, u32[]{:S(2)}, u32[]{:S(2)}) collective-permute-start(f32[1,32,1024]{2,1,0:T(8,128)S(1)} %get-tuple-element.9), channel_id=1, source_target_pairs={{0,1},{1,2},{2,3},{3,4},{4,5},{5,6},{6,7},{8,9},{9,10},{10,11},{11... | collective-permute-start | bytes 393224 | tf_op jit(solution)/shard_map/ppermute | solution.py:20
  306.2 1.3 copy-start.9
  307.6 24.8 %copy-start.15 = (f32[1,256]{1,0:T(1,128)S(1)}, f32[1,256]{1,0:T(1,128)}, u32[]{:S(2)}) copy-start(f32[1,256]{1,0:T(1,128)} %param.10) | copy-start | bytes 3076
  307.6 100.9 %copy-start.13 = (f32[1,256,128]{2,1,0:T(8,128)S(1)}, f32[1,256,128]{2,1,0:T(8,128)}, u32[]{:S(2)}) copy-start(f32[1,256,128]{2,1,0:T(8,128)} %param.13) | copy-start | bytes 393220
  308.0 11.6 %collective-permute-start.8 = (f32[1,256]{1,0:T(1,128)S(1)}, f32[1,256]{1,0:T(1,128)S(1)}, u32[]{:S(2)}, u32[]{:S(2)}) collective-permute-start(f32[1,256]{1,0:T(1,128)S(1)} %div.18), channel_id=1, source_target_pairs={{0,128},{8,136},{16,144},{24,152},{32,160},{40,168},{48,176},{56,1... | collective-permute-start | bytes 3080 | tf_op jit(solution)/shard_map/ppermute | solution.py:32
  320.2 10.3 %all-to-all-start = ((f32[8,1,256]{2,1,0:T(1,128)}), f32[8,1,256]{2,1,0:T(1,128)S(1)}, u32[]{:S(2)}, u32[]{:S(2)}) async-start(f32[8,1,256]{2,1,0:T(1,128)} %stack.2), calls=%async_computation | async-start | bytes 16384 | tf_op jit(solution)/shard_map/all_to_all | solution.py:106
Sparse Core Ops, SparseCore 0:
  16.5 239.7 all-reduce.10
